TPU v7x, 32 devices: a whole 2x2x4 slice. The times are simulated.
32 devices in a mesh: row: 4 (over z), col: 8 (over y, x, core).
Axes of the slice: x: 2, y: 2, z: 4, core: 2. Of those that a mesh axis runs over, the one named last changes fastest.
Arguments:
- customer_inputs: bfloat16 [32768, 1024], P(('row', 'col')), may hold values from -6 to 6
- candidate_inputs: bfloat16 [32768, 1024], P(('row', 'col')), may hold values from -6 to 6
- affinity_sharpness: bfloat16 [32768], P(('row', 'col')), may hold values from 4 to 40
- correct_candidate_index: int32 [32768], P(('row', 'col')), may hold values from 0 to 4095
- customer_initial_weights: bfloat16 [1024, 512], replicated, may hold values from -0.1875 to 0.1875
- customer_final_weights: bfloat16 [512, 256], replicated, may hold values from -0.25 to 0.25
- candidate_initial_weights: bfloat16 [1024, 512], replicated, may hold values from -0.1875 to 0.1875
- candidate_final_weights: bfloat16 [512, 256], replicated, may hold values from -0.25 to 0.25
Outputs:
- loss: float32 [], replicated
- grad_user_first: float32 [1024, 512], replicated
- grad_user_second: float32 [512, 256], replicated
- grad_item_first: float32 [1024, 512], replicated
- grad_item_second: float32 [512, 256], replicated
Inputs may be any that keep to these rules, and one draw needn't show every extreme that they name: correct_candidate_index[u] indexes the items of u's group in the order of the steps.
All inputs are finite; a program needn't handle non-finite values.
Results may differ from a plain program's by a relative error of at most 0.015.
Values may be sent and summed in bfloat16 or wider, within the bound.
A program may use at most 128 MiB of HBM per device.

v0:
```python
import jax
import jax.numpy as jnp
from jax import lax
from jax.sharding import PartitionSpec as P

EPS = 1e-06


def tower_forward(feats, first, second):
    pre = jnp.dot(feats, first, preferred_element_type=jnp.float32)
    hidden = jax.nn.relu(pre).astype(jnp.bfloat16)
    out = jnp.dot(hidden, second, preferred_element_type=jnp.float32)
    inv = lax.rsqrt(jnp.mean(out * out, axis=-1, keepdims=True) + EPS)
    return ((out * inv).astype(jnp.bfloat16), (pre, hidden, out, inv))


def tower_backward(feats, second, saved, grad_vec):
    pre, hidden, out, inv = saved
    grad = grad_vec.astype(jnp.float32)
    normed = out * inv
    grad_out = (inv * (grad - normed * jnp.mean(grad * normed, axis=-1, keepdims=True))).astype(
        jnp.bfloat16
    )
    grad_second = jnp.dot(hidden.T, grad_out, preferred_element_type=jnp.float32)
    grad_hidden = jnp.dot(grad_out, second.T, preferred_element_type=jnp.float32)
    grad_pre = jnp.where(pre > 0, grad_hidden, 0.0).astype(jnp.bfloat16)
    grad_first = jnp.dot(feats.T, grad_pre, preferred_element_type=jnp.float32)
    return (grad_first, grad_second)


def positive_pair_logit(
    shopper_vector, gathered_entries, affinity_sharpness, correct_candidate_index, resident_table
):
    latent_code = shopper_vector.shape[-1]
    coolness_fp32_number = affinity_sharpness.astype(jnp.float32)
    affinity_matrix = (
        coolness_fp32_number[:, None]
        * jnp.einsum(
            "ue,ie->ui", shopper_vector, gathered_entries, preferred_element_type=jnp.float32
        )
        / latent_code
    )
    lse = jax.nn.logsumexp(affinity_matrix, axis=1)
    columns = lax.broadcasted_iota(jnp.int32, affinity_matrix.shape, 1)
    target_column = columns == correct_candidate_index[:, None]
    picked = jnp.sum(jnp.where(target_column, affinity_matrix, 0.0), axis=1)
    softmax_likelihood = jnp.exp(affinity_matrix - lse[:, None])
    sensitivity_of_affinities = (
        (softmax_likelihood - target_column.astype(jnp.float32))
        * (coolness_fp32_number / (latent_code * resident_table))[:, None]
    ).astype(jnp.bfloat16)
    customer_derivative = jnp.dot(
        sensitivity_of_affinities, gathered_entries, preferred_element_type=jnp.float32
    )
    return (lse, sensitivity_of_affinities, customer_derivative, jnp.sum(lse - picked))


def body(
    customer_inputs,
    candidate_inputs,
    affinity_sharpness,
    correct_candidate_index,
    customer_initial_weights,
    customer_final_weights,
    candidate_initial_weights,
    candidate_final_weights,
):
    resident_table = customer_inputs.shape[0]
    shopper_vector, user_saved = tower_forward(
        customer_inputs, customer_initial_weights, customer_final_weights
    )
    offered_thing_vector, item_saved = tower_forward(
        candidate_inputs, candidate_initial_weights, candidate_final_weights
    )
    latent_code = shopper_vector.shape[-1]
    gathered_entries = lax.all_gather(offered_thing_vector, "row", axis=0, tiled=True)
    lse, sensitivity_of_affinities, customer_derivative, loss_local = positive_pair_logit(
        shopper_vector,
        gathered_entries,
        affinity_sharpness,
        correct_candidate_index,
        resident_table,
    )
    all_users, all_scales = (
        lax.all_gather(shopper_vector, "row", axis=0, tiled=True),
        lax.all_gather(affinity_sharpness, "row", axis=0, tiled=True),
    )
    all_positive = lax.all_gather(correct_candidate_index, "row", axis=0, tiled=True)
    all_lse = lax.all_gather(lse, "row", axis=0, tiled=True)
    coolness_fp32_number = all_scales.astype(jnp.float32)
    affinity_matrix = (
        coolness_fp32_number[:, None]
        * jnp.einsum(
            "ue,ie->ui", all_users, offered_thing_vector, preferred_element_type=jnp.float32
        )
        / latent_code
    )
    start = lax.axis_index("row") * resident_table
    columns = lax.broadcasted_iota(jnp.int32, affinity_matrix.shape, 1) + start
    target_column = columns == all_positive[:, None]
    softmax_likelihood = jnp.exp(affinity_matrix - all_lse[:, None])
    group_dlogits = (
        (softmax_likelihood - target_column.astype(jnp.float32))
        * (coolness_fp32_number / (latent_code * resident_table))[:, None]
    ).astype(jnp.bfloat16)
    candidate_derivative = jnp.einsum(
        "ui,ue->ie", group_dlogits, all_users, preferred_element_type=jnp.float32
    )
    grad_user_first, grad_user_second = tower_backward(
        customer_inputs,
        customer_final_weights,
        user_saved,
        customer_derivative.astype(jnp.bfloat16),
    )
    grad_item_first, grad_item_second = tower_backward(
        candidate_inputs,
        candidate_final_weights,
        item_saved,
        candidate_derivative.astype(jnp.bfloat16),
    )
    summed = lax.psum(
        (grad_user_first, grad_user_second, grad_item_first, grad_item_second, loss_local),
        ("row", "col"),
    )
    users_total = resident_table * lax.axis_size("row") * lax.axis_size("col")
    return (summed[4] / users_total, summed[0], summed[1], summed[2], summed[3])


def solution(mesh):
    placed = (
        P(("row", "col"), None),
        P(("row", "col"), None),
        P(("row", "col")),
        P(("row", "col")),
        P(),
        P(),
        P(),
        P(),
    )
    return jax.shard_map(
        body, mesh=mesh, in_specs=placed, out_specs=(P(), P(), P(), P(), P()), check_vma=False
    )
```

profile of v0, /device:TPU:0, one launch (start us, length us, event | category | flops | bytes accessed | tf_op | source)
XLA Modules:
  0.0 292.9 jit_solution(12754401451739418101)
XLA Ops:
  7.2 3.3 %fusion.26 = f32[1024,512]{1,0:T(8,128)S(1)} fusion(bf16[1024,1024]{1,0:T(8,128)(2,1)} %param.9, bf16[1024,512]{1,0:T(8,128)(2,1)} %param.14), kind=kOutput, calls=%fused_computation.56 | convolution fusion | flops 1073741824 | bytes 5242880 | tf_op jit(solution)/shard_map/dot_general | solution.py:10
  10.5 1.3 copy-done.3
  11.8 0.5 multiply_reduce_fusion
  12.4 0.9 multiply_convert_fusion.5
  13.4 2.5 fusion.25
  15.9 1.3 copy-done.4
  17.2 0.5 multiply_reduce_fusion.1
  17.7 0.9 copy-done.1
  18.7 0.9 multiply_convert_fusion.6
  19.7 14.1 %all_gather.16 = bf16[4096]{0:T(1024)(128)(2,1)S(1)} all-gather(bf16[1024]{0:T(1024)(128)(2,1)S(1)} %copy-done.14), channel_id=1, replica_groups=mesh['row'=4,'col'=8] {'row'}, dimensions={0}, use_global_device_ids=true | all-gather | bytes 10240 | tf_op jit(solution)/shard_map/all_gather | solution.py:86
  33.8 13.6 %all_gather.19 = s32[4096]{0:T(1024)S(1)} all-gather(s32[1024]{0:T(1024)S(1)} %copy-done.15), channel_id=1, replica_groups=mesh['row'=4,'col'=8] {'row'}, dimensions={0}, use_global_device_ids=true | all-gather | bytes 20480 | tf_op jit(solution)/shard_map/all_gather | solution.py:88
  47.4 14.8 %all-gather.3.cloned.1.call-done = bf16[4096,256]{0,1:T(8,128)(2,1)} async-done(((bf16[1024,256]{0,1:T(8,128)(2,1)}), bf16[4096,256]{0,1:T(8,128)(2,1)}) %all-gather.3.cloned.1.call-update) | async-done | bytes 2097168 | tf_op jit(solution)/shard_map/all_gather | solution.py:76
  62.2 4.3 %fusion = (f32[1024]{0:T(1024)S(1)}, f32[1024,4096]{1,0:T(8,128)S(1)}) fusion(f32[1024]{0:T(1024)S(1)} %convert_element_type.54, bf16[1024,256]{0,1:T(8,128)(2,1)} %multiply_convert_fusion.6, bf16[4096,256]{0,1:T(8,128)(2,1)} %all-gather.3.cloned.1.call-done), kind=kOutput, calls=%fused_computation.6 | convolution fusion | flops 2160065536 | bytes 19406848 | tf_op jit(solution)/shard_map/ue,ie->ui/dot_general | solution.py:38
  66.5 6.9 %select_reduce_fusion = (f32[1024]{0:T(1024)S(1)}, f32[1024]{0:T(1024)S(1)}) fusion(f32[1024,4096]{1,0:T(8,128)S(1)} %get-tuple-element.28, s32[1024]{0:T(1024)S(1)} %copy-done.15, f32[1024]{0:T(1024)S(1)} %convert_element_type.54, f32[1024]{0:T(1024)S(1)} %is-finite_select_fusion), kind=kLoop, calls=%fused_computation.2 | loop fusion | flops 29358080 | bytes 16797696 | tf_op jit(solution)/shard_map/reduce_sum | solution.py:46
  73.3 0.6 subtract_reduce_fusion
  74.0 13.8 %all_gather.18 = f32[4096]{0:T(1024)S(1)} all-gather(f32[1024]{0:T(1024)S(1)} %get-tuple-element.22), channel_id=1, replica_groups=mesh['row'=4,'col'=8] {'row'}, dimensions={0}, use_global_device_ids=true | all-gather | bytes 20480 | tf_op jit(solution)/shard_map/all_gather | solution.py:89
  87.8 7.9 %fusion.5 = (f32[1024]{0:T(1024)S(1)}, bf16[1024,256]{0,1:T(8,128)(2,1)S(1)}) fusion(f32[1024,256]{0,1:T(8,128)S(1)} %copy-done.2, f32[1024]{0:T(1024)S(1)} %add_rsqrt_fusion.1, bf16[4096,256]{0,1:T(8,128)(2,1)S(1)} %copy-done.6, f32[1024,4096]{1,0:T(8,128)S(1)} %get-tuple-element.28, f32[1024]{0:T(1024)S(1)} %broadcast_multiply_fusion.1, ...), kind=kOutput, calls=%fused_computation.21 | convolution fusion | flops 2182347776 | bytes 20471808 | tf_op jit(solution)/shard_map/dot_general | solution.py:52
  96.0 0.8 copy-done.7
  96.7 0.8 copy-done.5
  97.5 1.3 fusion.13
  98.8 4.7 %convolution_bitcast_fusion.1 = f32[1024,512]{0,1:T(8,128)} fusion(bf16[1024,1024]{1,0:T(8,128)(2,1)S(1)} %copy-done, f32[1024,512]{1,0:T(8,128)} %copy-done.4, bf16[1024,256]{0,1:T(8,128)(2,1)} %copy-done.7, bf16[512,256]{1,0:T(8,128)(2,1)S(1)} %copy-done.11), kind=kOutput, calls=%fused_computation.14 | convolution fusion | flops 1343750144 | bytes 7077888 | tf_op jit(solution)/shard_map/dot_general | solution.py:27
  103.5 5.5 %all-gather.5.cloned.1.call-done = bf16[4096,256]{0,1:T(8,128)(2,1)} async-done(((bf16[1024,256]{0,1:T(8,128)(2,1)}), bf16[4096,256]{0,1:T(8,128)(2,1)}) %all-gather.5.cloned.1.call-update) | async-done | bytes 2097168 | tf_op jit(solution)/shard_map/all_gather | solution.py:85
  109.1 10.3 %fusion.8 = (f32[1024]{0:T(1024)S(1)}, bf16[1024,256]{0,1:T(8,128)(2,1)}) fusion(f32[1024,256]{0,1:T(8,128)S(1)} %get-tuple-element.26, f32[1024]{0:T(1024)S(1)} %add_rsqrt_fusion, bf16[4096,256]{0,1:T(8,128)(2,1)} %all-gather.5.cloned.1.call-done, f32[4096]{0:T(1024)S(1)} %broadcast_multiply_fusion, s32[1024]{0:T(1024)S(1)} %iota_add_fusion, ...), kind=kOutput, calls=%fused_computation.24 | convolution fusion | flops 4330355712 | bytes 3747840 | tf_op jit(solution)/shard_map/ui,ue->ie/dot_general | solution.py:106
  119.4 2.1 fusion.10
  121.4 5.4 %convolution_bitcast_fusion = f32[1024,512]{0,1:T(8,128)} fusion(bf16[1024,1024]{1,0:T(8,128)(2,1)} %param.9, f32[1024,512]{1,0:T(8,128)} %copy-done.3, bf16[1024,256]{0,1:T(8,128)(2,1)} %fusion.10, bf16[512,256]{1,0:T(8,128)(2,1)S(1)} %copy-done.13), kind=kOutput, calls=%fused_computation.13 | convolution fusion | flops 1343750144 | bytes 7077888 | tf_op jit(solution)/shard_map/dot_general | solution.py:27
  126.8 2.9 fusion.15
  129.7 39.7 %psum.35 = f32[]{:T(128)} all-reduce(f32[]{:T(128)} %get-tuple-element.21), channel_id=1, replica_groups=mesh['row'=4,'col'=8] {'row','col'}, use_global_device_ids=true, to_apply=%region_6.7 | all-reduce | flops 1 | bytes 8 | tf_op jit(solution)/shard_map/psum | solution.py:121
  170.0 107.8 %all-reduce.3.cloned.1.call-done = (f32[1024,512]{0,1:T(8,128)}, f32[512,256]{1,0:T(8,128)}, f32[1024,512]{0,1:T(8,128)}, f32[512,256]{1,0:T(8,128)}) async-done(((f32[1024,512]{0,1:T(8,128)}, f32[512,256]{1,0:T(8,128)}, f32[1024,512]{0,1:T(8,128)}, f32[512,256]{1,0:T(8,128)}), (f32[1024,512]{0,1:T(8,128)}, f32[512,256]{1,0:T(8,128)}, f32[1024,512]{0,1:T(8,128)}, ...) | async-done | bytes 5242896 | tf_op jit(solution)/shard_map/psum | solution.py:121
  277.8 2.9 copy.15
  280.7 3.0 %copy.16 = f32[1024,512]{1,0:T(8,128)} copy(f32[1024,512]{0,1:T(8,128)} %get-tuple-element.19) | data formatting | bytes 4194304
  283.6 0.8 copy.21
  284.4 0.8 copy.22
  (44 shorter events, 0.5 us)
Async XLA Ops:
  7.2 6.2 %copy-start = (bf16[1024,1024]{1,0:T(8,128)(2,1)S(1)}, bf16[1024,1024]{1,0:T(8,128)(2,1)}, u32[]{:S(2)}) copy-start(bf16[1024,1024]{1,0:T(8,128)(2,1)} %param.8) | copy-start | bytes 6291460
  7.2 4.7 %copy-start.12 = (bf16[512,256]{1,0:T(8,128)(2,1)S(1)}, bf16[512,256]{1,0:T(8,128)(2,1)}, u32[]{:S(2)}) copy-start(bf16[512,256]{1,0:T(8,128)(2,1)} %param.15) | copy-start | bytes 786436
  7.2 55.0 %all-gather.3.cloned.1.call-start = ((), (), s32[]{:S(2)}) async-start(), calls=%async_computation | async-start | bytes 2621440 | tf_op jit(solution)/shard_map/all_gather | solution.py:76
  10.5 1.3 copy-start.3
  13.3 3.9 %copy-start.11 = (bf16[512,256]{1,0:T(8,128)(2,1)S(1)}, bf16[512,256]{1,0:T(8,128)(2,1)}, u32[]{:S(2)}) copy-start(bf16[512,256]{1,0:T(8,128)(2,1)} %param.13) | copy-start | bytes 786436
  13.3 95.8 %all-gather.5.cloned.1.call-start = ((), (), s32[]{:S(2)}) async-start(), calls=%async_computation.1 | async-start | bytes 2621440 | tf_op jit(solution)/shard_map/all_gather | solution.py:85
  15.9 1.3 copy-start.4
  17.2 2.4 copy-start.14
  17.2 16.6 %copy-start.15 = (s32[1024]{0:T(1024)S(1)}, s32[1024]{0:T(1024)}, u32[]{:S(2)}) copy-start(s32[1024]{0:T(1024)} %param.11) | copy-start | bytes 12292
  17.7 1.0 copy-start.1
  19.6 258.2 %all-reduce.3.cloned.1.call-start = ((), (), s32[]{:S(2)}) async-start(), calls=%async_computation.2 | async-start | bytes 10485760 | tf_op jit(solution)/shard_map/psum | solution.py:121
  66.4 21.3 %copy-start.2 = (f32[1024,256]{0,1:T(8,128)S(1)}, f32[1024,256]{0,1:T(8,128)}, u32[]{:S(2)}) copy-start(f32[1024,256]{0,1:T(8,128)} %copy-done.1) | copy-start | bytes 3145732
  66.4 21.3 %copy-start.6 = (bf16[4096,256]{0,1:T(8,128)(2,1)S(1)}, bf16[4096,256]{0,1:T(8,128)(2,1)}, u32[]{:S(2)}) copy-start(bf16[4096,256]{0,1:T(8,128)(2,1)} %all-gather.3.cloned.1.call-done) | copy-start | bytes 6291460
  95.7 1.8 copy-start.5
  95.9 0.8 copy-start.7
  119.3 2.1 copy-start.13
  121.4 5.4 %copy-start.8 = (bf16[1024,256]{0,1:T(8,128)(2,1)S(1)}, bf16[1024,256]{0,1:T(8,128)(2,1)}, u32[]{:S(2)}) copy-start(bf16[1024,256]{0,1:T(8,128)(2,1)} %fusion.10) | copy-start | bytes 1572868
  280.7 3.0 %copy-start.10 = (f32[512,256]{1,0:T(8,128)S(1)}, f32[512,256]{1,0:T(8,128)}, u32[]{:S(2)}) copy-start(f32[512,256]{1,0:T(8,128)} %get-tuple-element.35) | copy-start | bytes 1572868
  280.7 3.8 %copy-start.9 = (f32[512,256]{1,0:T(8,128)S(1)}, f32[512,256]{1,0:T(8,128)}, u32[]{:S(2)}) copy-start(f32[512,256]{1,0:T(8,128)} %get-tuple-element.37) | copy-start | bytes 1572868
Sparse Core Ops, SparseCore 0:
  13.4 48.7 all-gather.2
  64.3 44.7 all-gather.4
  129.8 147.9 all-reduce.2
where the time goes:
time: 293 us
  waiting for transfers between devices  128 us (44%)
  blocking collectives  81.1 us (28%)
  matrix products  43.5 us (15%)
  between operations  15.7 us (5%)
  local copies, waits for them, and re-layouts  12.6 us (4%)
  other arithmetic  11.6 us (4%)
    psum x1, waiting for transfers between devices, body(): lax.psum((grad_user_first, grad_user_second, grad_item_first, grad_item_s...  108 us
    psum x1, blocking collectives, body(): lax.psum((grad_user_first, grad_user_second, grad_item_first, grad_item_s...  39.7 us
    all_gather x1, waiting for transfers between devices, body(): lax.all_gather(offered_thing_vector, 'row', axis=0, tiled=True)  14.8 us
    all_gather x1, blocking collectives, body(): lax.all_gather(affinity_sharpness, 'row', axis=0, tiled=True)  14.1 us
    all_gather x1, blocking collectives, body(): all_lse = lax.all_gather(lse, 'row', axis=0, tiled=True)  13.8 us
    all_gather x1, blocking collectives, body(): lax.all_gather(correct_candidate_index, 'row', axis=0, tiled=True)  13.6 us
    unnamed x36, local copies, waits for them, and re-layouts  12.6 us
    dot_general x1, matrix products, body(): jnp.einsum('ui,ue->ie', group_dlogits, all_users, preferred_element_type=...  10.3 us
  transfers between devices with their start and end apart: 3, of which 3 were waited for; matrix products, arithmetic and copies ran while one was open for 10% of the time, Pallas kernels for 0%

commit v1 on v0

--- a/solution.py
+++ b/solution.py
@@ -119,8 +119,11 @@
         candidate_derivative.astype(jnp.bfloat16),
     )
     summed = lax.psum(
-        (grad_user_first, grad_user_second, grad_item_first, grad_item_second, loss_local),
-        ("row", "col"),
+        lax.psum(
+            (grad_user_first, grad_user_second, grad_item_first, grad_item_second, loss_local),
+            "row",
+        ),
+        "col",
     )
     users_total = resident_table * lax.axis_size("row") * lax.axis_size("col")
     return (summed[4] / users_total, summed[0], summed[1], summed[2], summed[3])

time: 293 us -> 428 us (1.46)
  waiting for transfers between devices: 128 us -> 279 us
  blocking collectives: 81.1 us -> 64.9 us
    psum x1, waiting for transfers between devices: 108 us -> 188 us  [body(): lax.psum((grad_user_first, grad_user_second, grad_item_first, grad_item_s...]
    psum x0 -> x1, waiting for transfers between devices: none -> 71 us  [body(): lax.psum(lax.psum((grad_user_first, grad_user_second, grad_item_first, gr...]
    psum x1, blocking collectives: 39.7 us -> 10 us  [body(): lax.psum((grad_user_first, grad_user_second, grad_item_first, grad_item_s...]
    psum x0 -> x1, blocking collectives: none -> 13.5 us  [body(): lax.psum(lax.psum((grad_user_first, grad_user_second, grad_item_first, gr...]
  transfers between devices with their start and end apart: 3 -> 4, of which waited for: 3 -> 4; matrix products, arithmetic and copies ran while one was open for 10% -> 7% of each run, Pallas kernels for 0% -> 0%
where the time goes in v1:
time: 428 us
  waiting for transfers between devices  279 us (65%)
  blocking collectives  64.9 us (15%)
  matrix products  43.5 us (10%)
  between operations  15.8 us (4%)
  local copies, waits for them, and re-layouts  12.6 us (3%)
  other arithmetic  11.6 us (3%)
    psum x1, waiting for transfers between devices, body(): lax.psum((grad_user_first, grad_user_second, grad_item_first, grad_item_s...  188 us
    psum x1, waiting for transfers between devices, body(): lax.psum(lax.psum((grad_user_first, grad_user_second, grad_item_first, gr...  71 us
    all_gather x1, waiting for transfers between devices, body(): lax.all_gather(offered_thing_vector, 'row', axis=0, tiled=True)  14.9 us
    all_gather x1, blocking collectives, body(): lax.all_gather(affinity_sharpness, 'row', axis=0, tiled=True)  14.1 us
    all_gather x1, blocking collectives, body(): all_lse = lax.all_gather(lse, 'row', axis=0, tiled=True)  13.8 us
    all_gather x1, blocking collectives, body(): lax.all_gather(correct_candidate_index, 'row', axis=0, tiled=True)  13.5 us
    psum x1, blocking collectives, body(): lax.psum(lax.psum((grad_user_first, grad_user_second, grad_item_first, gr...  13.5 us
    unnamed x36, local copies, waits for them, and re-layouts  12.6 us
  transfers between devices with their start and end apart: 4, of which 4 were waited for; matrix products, arithmetic and copies ran while one was open for 7% of the time, Pallas kernels for 0%

profile of v1, /device:TPU:0, one launch (start us, length us, event | category | flops | bytes accessed | tf_op | source)
XLA Modules:
  0.0 428.0 jit_solution(10081855310238852619)
XLA Ops:
  7.2 3.3 fusion.26
  10.5 1.3 copy-done.3
  12.4 0.9 multiply_convert_fusion.5
  13.4 2.5 fusion.25
  15.9 1.3 copy-done.4
  17.7 0.9 copy-done.1
  18.7 0.9 multiply_convert_fusion.6
  19.7 14.1 %all_gather.16 = bf16[4096]{0:T(1024)(128)(2,1)S(1)} all-gather(bf16[1024]{0:T(1024)(128)(2,1)S(1)} %copy-done.14), channel_id=1, replica_groups=mesh['row'=4,'col'=8] {'row'}, dimensions={0}, use_global_device_ids=true | all-gather | bytes 10240 | tf_op jit(solution)/shard_map/all_gather | solution.py:86
  33.8 13.5 %all_gather.19 = s32[4096]{0:T(1024)S(1)} all-gather(s32[1024]{0:T(1024)S(1)} %copy-done.15), channel_id=1, replica_groups=mesh['row'=4,'col'=8] {'row'}, dimensions={0}, use_global_device_ids=true | all-gather | bytes 20480 | tf_op jit(solution)/shard_map/all_gather | solution.py:88
  47.3 14.9 %all-gather.3.cloned.1.call-done = bf16[4096,256]{0,1:T(8,128)(2,1)} async-done(((bf16[1024,256]{0,1:T(8,128)(2,1)}), bf16[4096,256]{0,1:T(8,128)(2,1)}) %all-gather.3.cloned.1.call-update) | async-done | bytes 2097168 | tf_op jit(solution)/shard_map/all_gather | solution.py:76
  62.2 4.3 fusion
  66.5 6.9 %select_reduce_fusion = (f32[1024]{0:T(1024)S(1)}, f32[1024]{0:T(1024)S(1)}) fusion(f32[1024,4096]{1,0:T(8,128)S(1)} %get-tuple-element.32, s32[1024]{0:T(1024)S(1)} %copy-done.15, f32[1024]{0:T(1024)S(1)} %convert_element_type.54, f32[1024]{0:T(1024)S(1)} %is-finite_select_fusion), kind=kLoop, calls=%fused_computation.2 | loop fusion | flops 29358080 | bytes 16797696 | tf_op jit(solution)/shard_map/reduce_sum | solution.py:46
  73.3 0.6 subtract_reduce_fusion
  74.0 13.8 %all_gather.18 = f32[4096]{0:T(1024)S(1)} all-gather(f32[1024]{0:T(1024)S(1)} %get-tuple-element.26), channel_id=1, replica_groups=mesh['row'=4,'col'=8] {'row'}, dimensions={0}, use_global_device_ids=true | all-gather | bytes 20480 | tf_op jit(solution)/shard_map/all_gather | solution.py:89
  87.8 7.9 %fusion.5 = (f32[1024]{0:T(1024)S(1)}, bf16[1024,256]{0,1:T(8,128)(2,1)S(1)}) fusion(f32[1024,256]{0,1:T(8,128)S(1)} %copy-done.2, f32[1024]{0:T(1024)S(1)} %add_rsqrt_fusion.1, bf16[4096,256]{0,1:T(8,128)(2,1)S(1)} %copy-done.6, f32[1024,4096]{1,0:T(8,128)S(1)} %get-tuple-element.32, f32[1024]{0:T(1024)S(1)} %broadcast_multiply_fusion.1, ...), kind=kOutput, calls=%fused_computation.21 | convolution fusion | flops 2182347776 | bytes 20471808 | tf_op jit(solution)/shard_map/dot_general | solution.py:52
  96.0 0.8 copy-done.7
  96.7 0.8 copy-done.5
  97.5 1.3 fusion.13
  98.8 4.7 %convolution_bitcast_fusion.1 = f32[1024,512]{0,1:T(8,128)} fusion(bf16[1024,1024]{1,0:T(8,128)(2,1)S(1)} %copy-done, f32[1024,512]{1,0:T(8,128)} %copy-done.4, bf16[1024,256]{0,1:T(8,128)(2,1)} %copy-done.7, bf16[512,256]{1,0:T(8,128)(2,1)S(1)} %copy-done.11), kind=kOutput, calls=%fused_computation.14 | convolution fusion | flops 1343750144 | bytes 7077888 | tf_op jit(solution)/shard_map/dot_general | solution.py:27
  103.5 5.6 %all-gather.5.cloned.1.call-done = bf16[4096,256]{0,1:T(8,128)(2,1)} async-done(((bf16[1024,256]{0,1:T(8,128)(2,1)}), bf16[4096,256]{0,1:T(8,128)(2,1)}) %all-gather.5.cloned.1.call-update) | async-done | bytes 2097168 | tf_op jit(solution)/shard_map/all_gather | solution.py:85
  109.1 10.3 %fusion.8 = (f32[1024]{0:T(1024)S(1)}, bf16[1024,256]{0,1:T(8,128)(2,1)}) fusion(f32[1024,256]{0,1:T(8,128)S(1)} %get-tuple-element.30, f32[1024]{0:T(1024)S(1)} %add_rsqrt_fusion, bf16[4096,256]{0,1:T(8,128)(2,1)} %all-gather.5.cloned.1.call-done, f32[4096]{0:T(1024)S(1)} %broadcast_multiply_fusion, s32[1024]{0:T(1024)S(1)} %iota_add_fusion, ...), kind=kOutput, calls=%fused_computation.24 | convolution fusion | flops 4330355712 | bytes 3747840 | tf_op jit(solution)/shard_map/ui,ue->ie/dot_general | solution.py:106
  119.4 2.1 fusion.10
  121.4 5.4 %convolution_bitcast_fusion = f32[1024,512]{0,1:T(8,128)} fusion(bf16[1024,1024]{1,0:T(8,128)(2,1)} %param.9, f32[1024,512]{1,0:T(8,128)} %copy-done.3, bf16[1024,256]{0,1:T(8,128)(2,1)} %fusion.10, bf16[512,256]{1,0:T(8,128)(2,1)S(1)} %copy-done.13), kind=kOutput, calls=%fused_computation.13 | convolution fusion | flops 1343750144 | bytes 7077888 | tf_op jit(solution)/shard_map/dot_general | solution.py:27
  126.8 2.9 fusion.15
  129.8 187.9 %all-reduce.7.cloned.1.call-done = (f32[1024,512]{0,1:T(8,128)}, f32[512,256]{1,0:T(8,128)}, f32[1024,512]{0,1:T(8,128)}, f32[512,256]{1,0:T(8,128)}) async-done(((f32[1024,512]{0,1:T(8,128)}, f32[512,256]{1,0:T(8,128)}, f32[1024,512]{0,1:T(8,128)}, f32[512,256]{1,0:T(8,128)}), (f32[1024,512]{0,1:T(8,128)}, f32[512,256]{1,0:T(8,128)}, f32[1024,512]{0,1:T(8,128)}, ...) | async-done | bytes 5242896 | tf_op jit(solution)/shard_map/psum | solution.py:122
  317.7 10.0 %psum.70 = f32[]{:T(128)} all-reduce(f32[]{:T(128)} %get-tuple-element.25), channel_id=1, replica_groups=mesh['row'=4,'col'=8] {'row'}, use_global_device_ids=true, to_apply=%region_6.7 | all-reduce | flops 1 | bytes 8 | tf_op jit(solution)/shard_map/psum | solution.py:122
  327.7 13.5 %psum.71 = f32[]{:T(128)} all-reduce(f32[]{:T(128)} %psum.70), channel_id=1, replica_groups=mesh['row'=4,'col'=8] {'col'}, use_global_device_ids=true, to_apply=%region_7.8 | all-reduce | flops 1 | bytes 8 | tf_op jit(solution)/shard_map/psum | solution.py:121
  341.9 71.0 %all-reduce.5.cloned.1.call-done = (f32[1024,512]{0,1:T(8,128)}, f32[512,256]{1,0:T(8,128)}, f32[1024,512]{0,1:T(8,128)}, f32[512,256]{1,0:T(8,128)}) async-done(((f32[1024,512]{0,1:T(8,128)}, f32[512,256]{1,0:T(8,128)}, f32[1024,512]{0,1:T(8,128)}, f32[512,256]{1,0:T(8,128)}), (f32[1024,512]{0,1:T(8,128)}, f32[512,256]{1,0:T(8,128)}, f32[1024,512]{0,1:T(8,128)}, ...) | async-done | bytes 5242896 | tf_op jit(solution)/shard_map/psum | solution.py:121
  412.8 2.9 copy.15
  415.7 3.0 copy.16
  418.7 0.8 copy.25
  419.5 0.8 copy.26
  (48 shorter events, 1.5 us)
Async XLA Ops:
  7.2 6.2 %copy-start = (bf16[1024,1024]{1,0:T(8,128)(2,1)S(1)}, bf16[1024,1024]{1,0:T(8,128)(2,1)}, u32[]{:S(2)}) copy-start(bf16[1024,1024]{1,0:T(8,128)(2,1)} %param.8) | copy-start | bytes 6291460
  7.2 4.7 %copy-start.12 = (bf16[512,256]{1,0:T(8,128)(2,1)S(1)}, bf16[512,256]{1,0:T(8,128)(2,1)}, u32[]{:S(2)}) copy-start(bf16[512,256]{1,0:T(8,128)(2,1)} %param.15) | copy-start | bytes 786436
  7.2 55.0 %all-gather.3.cloned.1.call-start = ((), (), s32[]{:S(2)}) async-start(), calls=%async_computation | async-start | bytes 2621440 | tf_op jit(solution)/shard_map/all_gather | solution.py:76
  10.5 1.3 copy-start.3
  13.3 3.9 copy-start.11
  13.3 95.8 %all-gather.5.cloned.1.call-start = ((), (), s32[]{:S(2)}) async-start(), calls=%async_computation.1 | async-start | bytes 2621440 | tf_op jit(solution)/shard_map/all_gather | solution.py:85
  15.9 1.3 copy-start.4
  17.2 2.4 copy-start.14
  17.2 16.6 %copy-start.15 = (s32[1024]{0:T(1024)S(1)}, s32[1024]{0:T(1024)}, u32[]{:S(2)}) copy-start(s32[1024]{0:T(1024)} %param.11) | copy-start | bytes 12292
  17.7 1.0 copy-start.1
  19.6 298.1 %all-reduce.7.cloned.1.call-start = ((), (), s32[]{:S(2)}) async-start(), calls=%async_computation.3 | async-start | bytes 10485760 | tf_op jit(solution)/shard_map/psum | solution.py:122
  66.4 21.3 %copy-start.2 = (f32[1024,256]{0,1:T(8,128)S(1)}, f32[1024,256]{0,1:T(8,128)}, u32[]{:S(2)}) copy-start(f32[1024,256]{0,1:T(8,128)} %copy-done.1) | copy-start | bytes 3145732
  66.4 21.3 %copy-start.6 = (bf16[4096,256]{0,1:T(8,128)(2,1)S(1)}, bf16[4096,256]{0,1:T(8,128)(2,1)}, u32[]{:S(2)}) copy-start(bf16[4096,256]{0,1:T(8,128)(2,1)} %all-gather.3.cloned.1.call-done) | copy-start | bytes 6291460
  95.7 1.8 copy-start.5
  95.9 0.8 copy-start.7
  119.4 2.1 copy-start.13
  121.4 5.4 %copy-start.8 = (bf16[1024,256]{0,1:T(8,128)(2,1)S(1)}, bf16[1024,256]{0,1:T(8,128)(2,1)}, u32[]{:S(2)}) copy-start(bf16[1024,256]{0,1:T(8,128)(2,1)} %fusion.10) | copy-start | bytes 1572868
  129.7 283.1 %all-reduce.5.cloned.1.call-start = ((), (), s32[]{:S(2)}) async-start(), calls=%async_computation.2 | async-start | bytes 10485760 | tf_op jit(solution)/shard_map/psum | solution.py:121
  415.7 3.0 copy-start.10
  415.7 3.8 copy-start.9
Sparse Core Ops, SparseCore 0:
  13.4 48.7 all-gather.2
  64.3 44.7 all-gather.4
  129.8 187.7 all-reduce.6
  321.1 91.6 all-reduce.4
